TPU v7x, 32 devices: a whole 2x2x4 slice. The times are simulated.
32 devices in a mesh: groups: 2 (over x), space: 16 (over z, y, core).
Axes of the slice: x: 2, y: 2, z: 4, core: 2. Of those that a mesh axis runs over, the one named last changes fastest.
Arguments:
- eigvecs: bfloat16 [32, 64, 2, 3, 128], P('groups', 'space'), parts along dimension 0, may hold values from -1.3515625 to 1.3515625
- phase_index: int32 [128], P('groups'), parts along dimension 0, may hold values from 0 to 47
- perambulator: bfloat16 [512, 2, 128, 128], P(('groups', 'space')), parts along dimension 0, may hold values from -0.046875 to 0.046875
- tile_sink: int32 [512, 1], P(('groups', 'space')), parts along dimension 0, may hold values from 0 to 15; in each aligned block of 16 rows (0 to 15, 16 to 31, ...) at most 2 rows name the same one
- tile_sep: int32 [512], P(('groups', 'space')), parts along dimension 0, may hold values from 0 to 7
- tile_diagram: int32 [512], P(('groups', 'space')), parts along dimension 0, may hold values from 0 to 1
Outputs:
- elementals: bfloat16 [32, 2, 128, 128], P(('groups', 'space')), parts along dimension 0
- correlator: float32 [512, 2], P(('groups', 'space')), parts along dimension 0
There are 2 independent parts, one for each index of `groups`. A program takes and returns all parts, laid end to end along the dimension named above; each array names one. Nothing has to cross between parts.
Inputs may be any that keep to these rules, and one draw needn't show every extreme that they name: `tile_sink`: in the tiles of one device no sink time is named by more than 2 tiles.
All inputs are finite; a program needn't handle non-finite values.
Results may differ from a plain program's by a relative error of at most 0.0048.
Values may be sent and summed in bfloat16 or wider, within the bound.
A program may use at most 128 MiB of HBM per device.

v0:
```python
import math
import jax
import jax.numpy as jnp
from jax import lax
from jax.sharding import PartitionSpec as P

PERIOD = 48


def make_right(vecs, cosine, sine):
    real_part = vecs[..., 0, :, :].astype(jnp.float32)
    imag_part = vecs[..., 1, :, :].astype(jnp.float32)
    cos_col = cosine[:, None, None]
    sin_col = sine[:, None, None]
    first = (cos_col * real_part - sin_col * imag_part).astype(jnp.bfloat16)
    second = (sin_col * real_part + cos_col * imag_part).astype(jnp.bfloat16)
    top = jnp.stack([first, second], -2)
    bottom = jnp.stack([second, -first], -2)
    return jnp.stack([top, bottom], -4)


def phases(indices):
    angle = 2.0 * math.pi / PERIOD * indices.astype(jnp.float32)
    return (jnp.cos(angle), jnp.sin(angle))


def contract_tiles(sink_mat, source_mat, tiles, diagram):

    def mult(left, right):
        return jnp.einsum("bij,bjk->bik", left, right, preferred_element_type=jnp.float32)

    tile_re = tiles[:, 0]
    tile_im = tiles[:, 1]
    trans_re = jnp.swapaxes(tile_re, 1, 2)
    trans_im = -jnp.swapaxes(tile_im, 1, 2)
    flag = (diagram == 1)[:, None, None]
    left_re = jnp.where(flag, trans_re, tile_re)
    left_im = jnp.where(flag, trans_im, tile_im)
    right_re = jnp.where(flag, tile_re, trans_re)
    right_im = jnp.where(flag, tile_im, trans_im)
    sink_re = sink_mat[:, 0]
    sink_im = sink_mat[:, 1]
    src_re = jnp.swapaxes(source_mat[:, 0], 1, 2)
    src_im = -jnp.swapaxes(source_mat[:, 1], 1, 2)
    first_re = mult(sink_re, left_re) - mult(sink_im, left_im)
    first_im = mult(sink_re, left_im) + mult(sink_im, left_re)
    second_re = jnp.swapaxes(mult(src_re, right_re) - mult(src_im, right_im), 1, 2)
    second_im = jnp.swapaxes(mult(src_re, right_im) + mult(src_im, right_re), 1, 2)
    trace_re = jnp.sum(first_re * second_re - first_im * second_im, axis=(1, 2))
    trace_im = jnp.sum(first_re * second_im + first_im * second_re, axis=(1, 2))
    return jnp.stack([trace_re, trace_im], -1)


def run_blocks(step_fn, items, total):
    block = math.gcd(32, total)
    shaped = tuple((item.reshape((total // block, block) + item.shape[1:]) for item in items))
    result = lax.map(step_fn, shaped)
    return result.reshape((total,) + result.shape[2:])


def local(eigvecs, phase_index, perambulator, tile_sink, tile_sep, tile_diagram):
    tile_count = perambulator.shape[0]
    sinks = tile_sink[:, 0]
    cosine, sine = phases(phase_index)
    slices = lax.all_to_all(eigvecs, "space", split_axis=0, concat_axis=1, tiled=True)
    vecs = slices[0]
    right = make_right(vecs, cosine, sine)
    value = jnp.einsum("spck,spcol->okl", vecs, right, preferred_element_type=jnp.float32)
    elemental = value.astype(jnp.bfloat16)[None]
    gathered = lax.all_gather(elemental, "space", axis=0, tiled=True)
    time_count = gathered.shape[0]
    sources = jnp.mod(sinks - tile_sep, time_count)

    def holder_block(items):
        tiles, sink_ids, source_ids, diagram = items
        return contract_tiles(gathered[sink_ids], gathered[source_ids], tiles, diagram)

    correlator = run_blocks(holder_block, (perambulator, sinks, sources, tile_diagram), tile_count)
    return (elemental, correlator)


def solution(mesh):
    return jax.shard_map(
        local,
        mesh=mesh,
        in_specs=(
            P("groups", "space", None, None, None),
            P("groups"),
            P(("groups", "space"), None, None, None),
            P(("groups", "space"), None),
            P(("groups", "space")),
            P(("groups", "space")),
        ),
        out_specs=(P(("groups", "space"), None, None, None), P(("groups", "space"), None)),
        check_vma=False,
    )
```

profile of v0, /device:TPU:0, one launch (start us, length us, event | category | flops | bytes accessed | tf_op | source)
XLA Modules:
  0.0 76.8 jit_solution(16801960626893713510)
XLA Ops:
  7.2 0.0 copy-start.2
  7.2 0.0 copy-start
  7.2 7.6 %all-to-all-start = ((bf16[16,4,2,3,128]{4,2,3,1,0:T(2,128)(2,1)}), bf16[16,4,2,3,128]{4,2,3,1,0:T(2,128)(2,1)S(1)}, u32[]{:S(2)}, u32[]{:S(2)}) async-start(bf16[16,4,2,3,128]{4,2,3,1,0:T(2,128)(2,1)} %param.6), calls=%async_computation | async-start | bytes 196608 | tf_op jit(solution)/shard_map/all_to_all | solution.py:65
  14.7 0.0 all-gather.3.cloned.1.call-start
  14.8 0.0 copy-done.2
  14.9 7.3 %all-to-all-done = bf16[16,4,2,3,128]{4,2,3,1,0:T(2,128)(2,1)S(1)} async-done(((bf16[16,4,2,3,128]{4,2,3,1,0:T(2,128)(2,1)}), bf16[16,4,2,3,128]{4,2,3,1,0:T(2,128)(2,1)S(1)}, u32[]{:S(2)}, u32[]{:S(2)}) %all-to-all-start) | async-done | bytes 98336 | tf_op jit(solution)/shard_map/all_to_all | solution.py:65
  22.2 0.1 fusion.15
  22.3 0.1 fusion.21
  22.4 0.3 fusion
  22.6 0.7 copy.37
  23.4 0.0 all-gather.3.cloned.1.call-update
  23.4 0.0 copy-done
  23.4 0.1 slice_bitcast_fusion.5
  23.5 0.3 copy.40
  23.8 0.0 copy-start.4
  23.8 0.3 copy.42
  24.1 0.4 copy-done.4
  24.5 0.0 copy-start.3
  24.5 0.6 copy-done.3
  25.1 0.0 copy-start.5
  25.2 0.6 copy-done.5
  25.8 0.7 copy.49
  26.5 32.4 %all-gather.3.cloned.1.call-done = bf16[32,128,128]{2,1,0:T(8,128)(2,1)} async-done(((bf16[2,128,128]{2,1,0:T(8,128)(2,1)}), bf16[32,128,128]{2,1,0:T(8,128)(2,1)}) %all-gather.3.cloned.1.call-update) | async-done | bytes 1048592 | tf_op jit(solution)/shard_map/all_gather | solution.py:70
  59.0 2.9 %gather_fusion.1 = bf16[16,2,128,128]{3,2,1,0:T(8,128)(2,1)} fusion(bf16[16,2,128,128]{3,2,1,0:T(8,128)(2,1)} %bitcast.124, s32[1024]{0:T(1024)S(1)} %pad_clamp_fusion), kind=kCustom, calls=%fused_computation.1 | custom fusion | bytes 2097216 | tf_op jit(solution)/shard_map/while/body/eval_jaxpr/gather | solution.py:76
  61.9 2.0 %gather_fusion = bf16[16,2,128,128]{3,2,1,0:T(8,128)(2,1)S(1)} fusion(bf16[16,2,128,128]{3,2,1,0:T(8,128)(2,1)} %bitcast.125, s32[1024]{0:T(1024)S(1)} %pad_clamp_fusion.1), kind=kCustom, calls=%fused_computation | custom fusion | bytes 2097216 | tf_op jit(solution)/shard_map/while/body/eval_jaxpr/gather | solution.py:76
  63.9 1.5 %fusion.5 = f32[16,128,128]{2,1,0:T(8,128)S(1)} fusion(bf16[16,2,128,128]{3,2,1,0:T(8,128)(2,1)} %gather_fusion.1, pred[16]{0:T(512)(128)(4,1)S(1)} %broadcast_compare_fusion, bf16[16,128,128]{1,2,0:T(8,128)(2,1)S(1)} %copy.42, bf16[16,2,128,128]{3,2,1,0:T(8,128)(2,1)S(1)} %copy-done), kind=kOutput, calls=%fused_computation.24 | convolution fusion | flops 67633152 | bytes 2621952 | tf_op jit(solution)/shard_map/while/body/eval_jaxpr/bij,bjk->bik/dot_general | solution.py:30
  65.3 0.0 copy-start.1
  65.4 0.4 fusion.3
  65.7 0.8 %copy-done.1 = bf16[16,2,128,128]{3,2,1,0:T(8,128)(2,1)S(1)} copy-done((bf16[16,2,128,128]{3,2,1,0:T(8,128)(2,1)S(1)}, bf16[16,2,128,128]{3,2,1,0:T(8,128)(2,1)}, u32[]{:S(2)}) %copy-start.1) | copy-done | bytes 1048600
  66.6 0.4 fusion.6
  67.0 0.4 fusion.4
  67.4 0.4 convolution_add_fusion
  67.8 0.4 convolution_subtract_fusion
  68.2 0.4 convolution_subtract_fusion.1
  68.6 0.7 subtract_reduce_fusion
  69.3 0.6 pad_maximum_fusion
  (8 shorter events, 0.1 us)
Async XLA Ops:
  7.2 7.6 %copy-start.2 = (s32[64]{0:T(128)S(1)}, s32[64]{0:T(128)}, u32[]{:S(2)}) copy-start(s32[64]{0:T(128)} %param.7) | copy-start | bytes 772
  7.2 16.3 %copy-start = (bf16[16,2,128,128]{3,2,1,0:T(8,128)(2,1)S(1)}, bf16[16,2,128,128]{3,2,1,0:T(8,128)(2,1)}, u32[]{:S(2)}) copy-start(bf16[16,2,128,128]{3,2,1,0:T(8,128)(2,1)} %param.8) | copy-start | bytes 3145732
  7.2 14.9 %all-to-all-start = ((bf16[16,4,2,3,128]{4,2,3,1,0:T(2,128)(2,1)}), bf16[16,4,2,3,128]{4,2,3,1,0:T(2,128)(2,1)S(1)}, u32[]{:S(2)}, u32[]{:S(2)}) async-start(bf16[16,4,2,3,128]{4,2,3,1,0:T(2,128)(2,1)} %param.6), calls=%async_computation | async-start | bytes 196608 | tf_op jit(solution)/shard_map/all_to_all | solution.py:65
  14.7 44.2 %all-gather.3.cloned.1.call-start = ((), (), s32[]{:S(2)}) async-start(), calls=%async_computation.1 | async-start | bytes 1114112 | tf_op jit(solution)/shard_map/all_gather | solution.py:70
  23.8 0.7 copy-start.4
  24.5 0.7 copy-start.3
  25.1 0.7 copy-start.5
  65.3 1.2 %copy-start.1 = (bf16[16,2,128,128]{3,2,1,0:T(8,128)(2,1)S(1)}, bf16[16,2,128,128]{3,2,1,0:T(8,128)(2,1)}, u32[]{:S(2)}) copy-start(bf16[16,2,128,128]{3,2,1,0:T(8,128)(2,1)} %gather_fusion.1) | copy-start | bytes 3145732
Sparse Core Ops, SparseCore 0:
  23.5 35.3 all-gather.2
where the time goes:
time: 77.1 us; the launch traced here: 76.8 us
  waiting for transfers between devices  39.7 us (51%)
  between operations  14.2 us (18%)
  local copies, waits for them, and re-layouts  9.55 us (12%)
  starting transfers between devices  7.6 us (10%)
  matrix products  4.81 us (6%)
  other arithmetic  0.85 us (1%)
    all_gather x1, waiting for transfers between devices, local(): gathered = lax.all_gather(elemental, 'space', axis=0, tiled=True)  32.4 us
    all_to_all x1, starting transfers between devices, local(): lax.all_to_all(eigvecs, 'space', split_axis=0, concat_axis=1, tiled=True)  7.56 us
    all_to_all x1, waiting for transfers between devices, local(): lax.all_to_all(eigvecs, 'space', split_axis=0, concat_axis=1, tiled=True)  7.27 us
    dot_general x8, matrix products, mult(): jnp.einsum('bij,bjk->bik', left, right, preferred_element_type=jnp.float32)  4.56 us
    unnamed x13, local copies, waits for them, and re-layouts  3.24 us
    gather x1, local copies, waits for them, and re-layouts, holder_block(): gathered[source_ids]  2.92 us
    gather x1, local copies, waits for them, and re-layouts, holder_block(): gathered[sink_ids]  1.97 us
  transfers between devices with their start and end apart: 2, of which 2 were waited for; matrix products, arithmetic and copies ran while one was open for 2% of the time, Pallas kernels for 0%

commit v1 on v0

--- a/solution.py
+++ b/solution.py
@@ -1,3 +1,4 @@
+import functools
 import math
 import jax
 import jax.numpy as jnp
@@ -5,6 +6,16 @@
 from jax.sharding import PartitionSpec as P
 
 PERIOD = 48
+
+
+def produce_halves_on_mesh(row_data, which_axis, where_dim):
+    parts_out = jnp.stack([row_data for _ in range(lax.axis_size(which_axis))])
+    new = lax.all_to_all(parts_out, which_axis, split_axis=0, concat_axis=0)
+    mixed_arr = jnp.concatenate(new, where_dim)
+    return mixed_arr
+
+
+match_digits = functools.partial(produce_halves_on_mesh, which_axis="space", where_dim=0)
 
 
 def make_right(vecs, cosine, sine):
@@ -67,7 +78,7 @@
     right = make_right(vecs, cosine, sine)
     value = jnp.einsum("spck,spcol->okl", vecs, right, preferred_element_type=jnp.float32)
     elemental = value.astype(jnp.bfloat16)[None]
-    gathered = lax.all_gather(elemental, "space", axis=0, tiled=True)
+    gathered = match_digits(elemental)
     time_count = gathered.shape[0]
     sources = jnp.mod(sinks - tile_sep, time_count)
 

time: 77.1 us -> 55 us (0.71)
  the two profiles are of different devices: /device:TPU:0 before, /device:TPU:11 now
where the time goes in v1:
time: 55 us; the launch traced here: 54.6 us
  waiting for transfers between devices  25.7 us (47%)
  starting transfers between devices  12.2 us (22%)
  local copies, waits for them, and re-layouts  10.1 us (18%)
  matrix products  4.89 us (9%)
  other arithmetic  0.85 us (2%)
  between operations  0.83 us (2%)
    all_to_all x1, waiting for transfers between devices, produce_halves_on_mesh(): new = lax.all_to_all(parts_out, which_axis, split_axis=0, concat_axis=0)  20.3 us
    all_to_all x1, starting transfers between devices, local(): lax.all_to_all(eigvecs, 'space', split_axis=0, concat_axis=1, tiled=True)  6.59 us
    all_to_all x1, starting transfers between devices, produce_halves_on_mesh(): new = lax.all_to_all(parts_out, which_axis, split_axis=0, concat_axis=0)  5.62 us
    all_to_all x1, waiting for transfers between devices, local(): lax.all_to_all(eigvecs, 'space', split_axis=0, concat_axis=1, tiled=True)  5.4 us
    dot_general x8, matrix products, mult(): jnp.einsum('bij,bjk->bik', left, right, preferred_element_type=jnp.float32)  4.63 us
    unnamed x15, local copies, waits for them, and re-layouts  2.87 us
    gather x1, local copies, waits for them, and re-layouts, holder_block(): gathered[sink_ids]  1.7 us
    gather x1, local copies, waits for them, and re-layouts, holder_block(): gathered[source_ids]  1.65 us
  transfers between devices with their start and end apart: 2, of which 2 were waited for; matrix products, arithmetic and copies ran while one was open for 6% of the time, Pallas kernels for 0%

profile of v1, /device:TPU:11, one launch (start us, length us, event | category | flops | bytes accessed | tf_op | source)
XLA Modules:
  0.0 54.6 jit_solution(18197460929390654230)
XLA Ops:
  0.6 0.0 copy-start.3
  0.6 6.6 %all-to-all-start = ((bf16[16,4,2,3,128]{4,2,3,1,0:T(2,128)(2,1)}), bf16[16,4,2,3,128]{4,2,3,1,0:T(2,128)(2,1)S(1)}, u32[]{:S(2)}, u32[]{:S(2)}) async-start(bf16[16,4,2,3,128]{4,2,3,1,0:T(2,128)(2,1)} %param.6), calls=%async_computation | async-start | bytes 196608 | tf_op jit(solution)/shard_map/all_to_all | solution.py:76
  7.2 0.0 copy-done.3
  7.3 5.4 %all-to-all-done = bf16[16,4,2,3,128]{4,2,3,1,0:T(2,128)(2,1)S(1)} async-done(((bf16[16,4,2,3,128]{4,2,3,1,0:T(2,128)(2,1)}), bf16[16,4,2,3,128]{4,2,3,1,0:T(2,128)(2,1)S(1)}, u32[]{:S(2)}, u32[]{:S(2)}) %all-to-all-start) | async-done | bytes 98336 | tf_op jit(solution)/shard_map/all_to_all | solution.py:76
  12.7 0.1 fusion.15
  12.8 0.1 fusion.21
  12.9 0.3 fusion
  13.2 0.1 copy.37
  13.3 1.2 %stack.39 = bf16[16,1,2,128,128]{4,3,2,1,0:T(8,128)(2,1)} broadcast(bf16[2,128,128]{2,1,0:T(8,128)(2,1)S(1)} %copy.37), dimensions={2,3,4} | broadcast | bytes 1114112 | tf_op jit(solution)/shard_map/stack | solution.py:12
  14.6 0.0 copy-start
  14.6 5.6 %all-to-all-start.1 = ((bf16[16,1,2,128,128]{4,3,2,1,0:T(8,128)(2,1)}), bf16[16,1,2,128,128]{4,3,2,1,0:T(8,128)(2,1)S(1)}, u32[]{:S(2)}, u32[]{:S(2)}) async-start(bf16[16,1,2,128,128]{4,3,2,1,0:T(8,128)(2,1)} %stack.39), calls=%async_computation.1 | async-start | bytes 2097152 | tf_op jit(solution)/shard_map/all_to_all | solution.py:13
  20.2 0.0 copy-done
  20.2 0.9 %slice_bitcast_fusion.5 = (bf16[16,128,128]{2,1,0:T(8,128)(2,1)S(1)}, bf16[16,128,128]{2,1,0:T(8,128)(2,1)}) fusion(bf16[16,2,128,128]{3,2,1,0:T(8,128)(2,1)S(1)} %copy-done), kind=kLoop, calls=%fused_computation.21 | loop fusion | bytes 2097152 | tf_op jit(solution)/shard_map/while/body/eval_jaxpr/squeeze | solution.py:43
  21.1 0.3 copy.40
  21.4 0.0 copy-start.5
  21.4 1.3 %copy.42 = bf16[16,128,128]{1,2,0:T(8,128)(2,1)S(1)} copy(bf16[16,128,128]{2,1,0:T(8,128)(2,1)} %get-tuple-element.34) | data formatting | bytes 1048576 | tf_op jit(solution)/shard_map/while/body/eval_jaxpr/squeeze | solution.py:44
  22.7 0.0 copy-done.5
  22.8 0.0 copy-start.4
  22.8 0.6 %copy-done.4 = s32[16]{0:T(128)S(1)} copy-done((s32[16]{0:T(128)S(1)}, s32[16]{0:T(128)}, u32[]{:S(2)}) %copy-start.4) | copy-done | bytes 88
  23.4 0.0 copy-start.6
  23.5 0.6 %copy-done.6 = s32[16]{0:T(128)S(1)} copy-done((s32[16]{0:T(128)S(1)}, s32[16]{0:T(128)}, u32[]{:S(2)}) %copy-start.6) | copy-done | bytes 88
  24.1 0.7 %copy.49 = bf16[1,2,128,128]{3,2,1,0:T(8,128)(2,1)} copy(bf16[1,2,128,128]{2,3,1,0:T(8,128)(2,1)S(1)} %bitcast.130) | data formatting | bytes 131072
  24.8 20.3 %all-to-all-done.1 = bf16[16,1,2,128,128]{4,3,2,1,0:T(8,128)(2,1)S(1)} async-done(((bf16[16,1,2,128,128]{4,3,2,1,0:T(8,128)(2,1)}), bf16[16,1,2,128,128]{4,3,2,1,0:T(8,128)(2,1)S(1)}, u32[]{:S(2)}, u32[]{:S(2)}) %all-to-all-start.1) | async-done | bytes 1048608 | tf_op jit(solution)/shard_map/all_to_all | solution.py:13
  45.1 1.7 %gather_fusion.1 = bf16[16,2,128,128]{3,2,1,0:T(8,128)(2,1)} fusion(bf16[16,2,128,128]{3,2,1,0:T(8,128)(2,1)S(1)} %bitcast.124, s32[1024]{0:T(1024)S(1)} %pad_clamp_fusion), kind=kCustom, calls=%fused_computation.1 | custom fusion | bytes 2097216 | tf_op jit(solution)/shard_map/while/body/eval_jaxpr/gather | solution.py:87
  46.8 1.7 %gather_fusion = bf16[16,2,128,128]{3,2,1,0:T(8,128)(2,1)} fusion(bf16[16,2,128,128]{3,2,1,0:T(8,128)(2,1)S(1)} %bitcast.125, s32[1024]{0:T(1024)S(1)} %pad_clamp_fusion.1), kind=kCustom, calls=%fused_computation | custom fusion | bytes 2097216 | tf_op jit(solution)/shard_map/while/body/eval_jaxpr/gather | solution.py:87
  48.5 0.0 copy-start.1
  48.5 1.5 %fusion.5 = f32[16,128,128]{2,1,0:T(8,128)S(1)} fusion(bf16[16,2,128,128]{3,2,1,0:T(8,128)(2,1)} %gather_fusion.1, pred[16]{0:T(512)(128)(4,1)S(1)} %broadcast_compare_fusion, bf16[16,128,128]{1,2,0:T(8,128)(2,1)S(1)} %copy.42, bf16[16,2,128,128]{3,2,1,0:T(8,128)(2,1)S(1)} %copy-done), kind=kOutput, calls=%fused_computation.24 | convolution fusion | flops 67633152 | bytes 2621952 | tf_op jit(solution)/shard_map/while/body/eval_jaxpr/bij,bjk->bik/dot_general | solution.py:41
  50.0 0.0 copy-done.1
  50.0 0.0 copy-start.2
  50.1 0.4 fusion.3
  50.4 0.8 %copy-done.2 = bf16[16,2,128,128]{3,2,1,0:T(8,128)(2,1)S(1)} copy-done((bf16[16,2,128,128]{3,2,1,0:T(8,128)(2,1)S(1)}, bf16[16,2,128,128]{3,2,1,0:T(8,128)(2,1)}, u32[]{:S(2)}) %copy-start.2) | copy-done | bytes 1048600
  51.3 0.4 fusion.6
  51.7 0.4 fusion.4
  52.1 0.4 convolution_add_fusion
  52.5 0.4 convolution_subtract_fusion
  52.9 0.4 convolution_subtract_fusion.1
  53.3 0.7 %subtract_reduce_fusion = (f32[16]{0:T(128)S(1)}, f32[16]{0:T(128)S(1)}) fusion(f32[16,128,128]{2,1,0:T(8,128)S(1)} %convolution_add_fusion, f32[16,128,128]{2,1,0:T(8,128)S(1)} %convolution_subtract_fusion.1, f32[16,128,128]{2,1,0:T(8,128)S(1)} %convolution_subtract_fusion, f32[16,128,128]{2,1,0:T(8,128)S(1)} %fusion.3, ...), kind=kOutput, calls=%fused_computation.9 | convolution fusion | flops 69730272 | bytes 5767808 | tf_op jit(solution)/shard_map/while/body/eval_jaxpr/bij,bjk->bik/dot_general | solution.py:41
  54.0 0.6 %pad_maximum_fusion = f32[16,2]{0,1:T(2,128)} fusion(f32[16,1]{0,1:T(1,128)S(1)} %bitcast.132, f32[16,1]{0,1:T(1,128)S(1)} %bitcast.131), kind=kLoop, calls=%fused_computation.48 | loop fusion | flops 32 | bytes 256 | tf_op jit(solution)/shard_map/while/body/eval_jaxpr/stack | solution.py:62
  (8 shorter events, 0.1 us)
Async XLA Ops:
  0.6 6.6 %copy-start.3 = (s32[64]{0:T(128)S(1)}, s32[64]{0:T(128)}, u32[]{:S(2)}) copy-start(s32[64]{0:T(128)} %param.7) | copy-start | bytes 772
  0.6 12.0 %all-to-all-start = ((bf16[16,4,2,3,128]{4,2,3,1,0:T(2,128)(2,1)}), bf16[16,4,2,3,128]{4,2,3,1,0:T(2,128)(2,1)S(1)}, u32[]{:S(2)}, u32[]{:S(2)}) async-start(bf16[16,4,2,3,128]{4,2,3,1,0:T(2,128)(2,1)} %param.6), calls=%async_computation | async-start | bytes 196608 | tf_op jit(solution)/shard_map/all_to_all | solution.py:76
  14.6 5.6 %copy-start = (bf16[16,2,128,128]{3,2,1,0:T(8,128)(2,1)S(1)}, bf16[16,2,128,128]{3,2,1,0:T(8,128)(2,1)}, u32[]{:S(2)}) copy-start(bf16[16,2,128,128]{3,2,1,0:T(8,128)(2,1)} %param.8) | copy-start | bytes 3145732
  14.6 30.6 %all-to-all-start.1 = ((bf16[16,1,2,128,128]{4,3,2,1,0:T(8,128)(2,1)}), bf16[16,1,2,128,128]{4,3,2,1,0:T(8,128)(2,1)S(1)}, u32[]{:S(2)}, u32[]{:S(2)}) async-start(bf16[16,1,2,128,128]{4,3,2,1,0:T(8,128)(2,1)} %stack.39), calls=%async_computation.1 | async-start | bytes 2097152 | tf_op jit(solution)/shard_map/all_to_all | solution.py:13
  21.4 1.3 %copy-start.5 = (s32[16,1]{0,1:T(1,128)S(1)}, s32[16,1]{0,1:T(1,128)}, u32[]{:S(2)}) copy-start(s32[16,1]{0,1:T(1,128)} %param.9) | copy-start | bytes 196
  22.8 0.7 %copy-start.4 = (s32[16]{0:T(128)S(1)}, s32[16]{0:T(128)}, u32[]{:S(2)}) copy-start(s32[16]{0:T(128)} %param.10) | copy-start | bytes 196
  23.4 0.7 %copy-start.6 = (s32[16]{0:T(128)S(1)}, s32[16]{0:T(128)}, u32[]{:S(2)}) copy-start(s32[16]{0:T(128)} %param.11) | copy-start | bytes 196
  48.5 1.6 %copy-start.1 = (bf16[16,2,128,128]{3,2,1,0:T(8,128)(2,1)S(1)}, bf16[16,2,128,128]{3,2,1,0:T(8,128)(2,1)}, u32[]{:S(2)}) copy-start(bf16[16,2,128,128]{3,2,1,0:T(8,128)(2,1)} %gather_fusion) | copy-start | bytes 3145732
  50.0 1.2 %copy-start.2 = (bf16[16,2,128,128]{3,2,1,0:T(8,128)(2,1)S(1)}, bf16[16,2,128,128]{3,2,1,0:T(8,128)(2,1)}, u32[]{:S(2)}) copy-start(bf16[16,2,128,128]{3,2,1,0:T(8,128)(2,1)} %gather_fusion.1) | copy-start | bytes 3145732
